TPU v7x, 512 devices: a whole 4x8x8 slice. The times are simulated.
512 devices in a mesh: grp: 4 (over z_hi, core), wide: 128 (over z_lo, x, y).
Axes of the slice: x: 4, y: 8, z: 8 (z_hi: 2, z_lo: 4; z = z_hi * 4 + z_lo), core: 2. Of those that a mesh axis runs over, the one named last changes fastest.
Arguments:
- images: bfloat16 [2048, 256, 2048], P(('grp', 'wide')), may hold values from -6 to 6
- legendre_real: float32 [128, 128], replicated, may hold values from -0.375 to 0.375
- legendre_imag: float32 [128, 128], replicated, may hold values from -0.375 to 0.375
- amplitudes: float32 [128, 256, 128], P('wide'), may hold values from -6 to 6
Outputs:
- projected: float32 [128, 256, 128], P('wide', 'grp')
All inputs are finite; a program needn't handle non-finite values.
Results may differ from a plain program's by a relative error of at most 0.0023.
Values may be sent and summed in bfloat16 or wider, within the bound.
No kernel may reach another device: no remote copies, remote signals or barrier semaphores. Data moves between devices by JAX's collectives and lax.ppermute only.
A program may use at most 64 MiB of HBM per device.

v0:
```python
import math
import jax
import jax.numpy as jnp
from jax import lax
from jax.sharding import PartitionSpec as P

HARMS = 128


def harmonic_rows(points, count):
    angle_idx = jnp.arange(points, dtype=jnp.int32)
    harm_idx = jnp.arange(count, dtype=jnp.int32)
    product = harm_idx[:, None] * angle_idx[None, :] % points
    phase = product.astype(jnp.float32) * (2.0 * math.pi / points)
    norm_scale = 1.0 / math.sqrt(points)
    both = jnp.stack([jnp.cos(phase) * norm_scale, -jnp.sin(phase) * norm_scale], axis=1)
    return both.reshape(count * 2, points).astype(jnp.bfloat16)


def invert_harms(stacked, legendre_real, legendre_imag):
    result = jnp.dot(legendre_real, stacked[:, 0], precision=lax.Precision.HIGHEST)
    return result + jnp.dot(legendre_imag, stacked[:, 1], precision=lax.Precision.HIGHEST)


def body(images, legendre_real, legendre_imag, amplitudes):
    local_img, radii, points = images.shape
    table_rows = harmonic_rows(points, HARMS)
    flat_images = images.reshape(local_img * radii, points)
    spectra = lax.dot_general(
        table_rows, flat_images, (((1,), (1,)), ((), ())), preferred_element_type=jnp.float32
    )
    spectra = spectra.astype(jnp.bfloat16).reshape(HARMS, 2, local_img, radii)
    pooled = lax.all_to_all(spectra, "wide", split_axis=0, concat_axis=2, tiled=True)
    total_img = pooled.shape[2] * lax.axis_size("grp")
    gram = jnp.einsum("kanr,kbns->kabrs", pooled, pooled, preferred_element_type=jnp.float32)
    real_part = (gram[:, 0, 0] + gram[:, 1, 1]) / total_img
    imag_part = (gram[:, 1, 0] - gram[:, 0, 1]) / total_img
    corr = jnp.stack([real_part, imag_part], axis=1)
    own_harms = corr.shape[0]
    own_degrees = amplitudes.shape[0]
    groups = lax.axis_size("grp")
    summed = lax.psum_scatter(corr, "grp", scatter_dimension=2, tiled=True)
    flat = summed.reshape(own_harms, 2, radii // groups * radii)
    every_harm = lax.all_to_all(flat, "wide", split_axis=2, concat_axis=0, tiled=True)
    degree_part = invert_harms(every_harm, legendre_real, legendre_imag)
    mine = lax.all_to_all(degree_part, "wide", split_axis=0, concat_axis=1, tiled=True)
    inverted = mine.reshape(own_degrees, radii // groups, radii)
    return jnp.einsum("lrs,lsk->lrk", inverted, amplitudes, precision=lax.Precision.HIGHEST)


def solution(mesh):
    return jax.shard_map(
        body,
        mesh=mesh,
        in_specs=(P(("grp", "wide"), None, None), P(), P(), P("wide", None, None)),
        out_specs=P("wide", "grp", None),
        check_vma=False,
    )
```

profile of v0, /device:TPU:2, one launch (start us, length us, event | category | flops | bytes accessed | tf_op | source)
XLA Modules:
  0.0 285.0 jit_solution(9286189481164600383)
XLA Ops:
  6.5 0.0 copy-start
  6.5 0.0 all-reduce.3.cloned.1.call-start
  6.5 4.3 %multiply_convert_fusion = (bf16[128,1,2048]{2,0,1:T(8,128)(2,1)S(1)}, bf16[128,1,2048]{2,0,1:T(8,128)(2,1)S(1)}) fusion(), kind=kLoop, calls=%fused_computation.12 | loop fusion | flops 4980736 | bytes 1048576 | tf_op jit(solution)/shard_map/convert.1
  10.9 0.1 pad_maximum_fusion
  11.0 1.1 copy.43
  12.1 0.4 convert_element_type.30
  12.5 3.5 %convolution_convert_fusion = bf16[256,1024]{1,0:T(8,128)(2,1)S(1)} fusion(bf16[256,2048]{1,0:T(8,128)(2,1)S(1)} %convert_element_type.30, bf16[1024,2048]{1,0:T(8,128)(2,1)} %bitcast.73), kind=kOutput, calls=%fused_computation.4 | convolution fusion | flops 1074003968 | bytes 5767168 | tf_op jit(solution)/shard_map/dot_general | solution.py:29
  16.0 0.4 reshape.176
  16.4 35.2 %all_to_all.46 = bf16[128,2,4,256]{3,2,1,0:T(4,128)(2,1)S(1)} all-to-all(bf16[128,2,4,256]{3,2,1,0:T(4,128)(2,1)S(1)} %reshape.176), channel_id=1, replica_groups=mesh['grp'=4,'wide'=128] {'wide'}, dimensions={0} | all-to-all | bytes 1048576 | tf_op jit(solution)/shard_map/all_to_all | solution.py:33
  51.6 0.5 copy.55
  52.0 0.5 convolution_bitcast_fusion
  52.7 1.0 copy.49
  53.7 0.0 all-reduce.3.cloned.1.call-update
  53.7 1.3 dynamic-slice
  55.6 59.9 %all-reduce.3.cloned.1.call-done = f32[1,2,256,256]{3,1,0,2:T(2,128)} async-done(((f32[1,2,256,256]{3,1,0,2:T(2,128)}), f32[1,2,256,256]{3,1,0,2:T(2,128)}) %all-reduce.3.cloned.1.call-update) | async-done | bytes 524304
  115.6 0.9 constant_dynamic-slice_fusion
  116.5 12.0 %copy.50 = f32[1,2,16384]{1,0,2:T(1,128)} copy(f32[1,2,16384]{2,1,0:T(2,128)S(1)} %bitcast.70) | data formatting | bytes 262144 | tf_op jit(solution)/shard_map/reshape | solution.py:43
  128.5 0.5 broadcast.138
  129.0 74.5 %reduce.4 = f32[16384,2]{1,0:T(8,128)} reduce(f32[16384,1,2]{2,1,0:T(1,128)} %bitcast.68, f32[]{:T(128)} %broadcast.138), dimensions={1}, to_apply=%bitcast.61.reduce_sub_computation | reduce | bytes 262148
  203.5 7.6 %reshape.194 = f32[128,1,256]{2,1,0:T(1,128)S(1)} reshape(f32[16384,2]{1,0:T(8,128)} %reduce.4) | data formatting | bytes 262144
  211.1 24.9 %all_to_all.47 = f32[128,1,256]{2,1,0:T(1,128)S(1)} all-to-all(f32[128,1,256]{2,1,0:T(1,128)S(1)} %reshape.194), channel_id=1, replica_groups=mesh['grp'=4,'wide'=128] {'wide'}, dimensions={0} | all-to-all | bytes 262144 | tf_op jit(solution)/shard_map/all_to_all | solution.py:44
  236.0 1.0 reduce.5
  236.9 14.9 %reshape.195 = f32[16384,1,2]{2,1,0:T(1,128)} reshape(f32[128,256]{1,0:T(8,128)S(1)} %reduce.5) | data formatting | bytes 262144
  251.8 5.2 %copy.56 = f32[1,2,128,128]{3,2,1,0:T(8,128)S(1)} copy(f32[1,2,128,128]{1,3,2,0:T(8,128)} %bitcast.69) | data formatting | bytes 262144 | tf_op jit(solution)/shard_map/all_to_all | solution.py:44
  257.1 0.3 fusion.16
  257.4 0.3 fusion
  257.7 0.1 copy.52
  257.8 18.1 %all_to_all.48 = f32[128,1,128]{2,1,0:T(1,128)S(1)} all-to-all(f32[128,1,128]{2,1,0:T(1,128)S(1)} %copy.52), channel_id=1, replica_groups=mesh['grp'=4,'wide'=128] {'wide'}, dimensions={0} | all-to-all | bytes 131072 | tf_op jit(solution)/shard_map/all_to_all | solution.py:46
  275.9 0.5 broadcast.137
  276.4 0.8 reduce.3
  277.3 0.0 copy-done
  277.3 0.8 convolution_bitcast_fusion.1
  (8 shorter events, 0.1 us)
Async XLA Ops:
  6.5 270.7 %copy-start = (f32[1,256,128]{2,1,0:T(8,128)S(1)}, f32[1,256,128]{2,1,0:T(8,128)}, u32[]{:S(2)}) copy-start(f32[1,256,128]{2,1,0:T(8,128)} %param.7) | copy-start | bytes 393220
  6.5 109.0 %all-reduce.3.cloned.1.call-start = ((), (), s32[]{:S(2)}) async-start(), calls=%async_computation.3 | async-start | bytes 1048576
  251.8 5.3 %copy-start.1 = (f32[128,128]{1,0:T(8,128)S(1)}, f32[128,128]{1,0:T(8,128)}, u32[]{:S(2)}) copy-start(f32[128,128]{1,0:T(8,128)} %param.5) | copy-start | bytes 196612
  251.8 5.6 %copy-start.2 = (f32[128,128]{1,0:T(8,128)S(1)}, f32[128,128]{1,0:T(8,128)}, u32[]{:S(2)}) copy-start(f32[128,128]{1,0:T(8,128)} %param.6) | copy-start | bytes 196612
Sparse Core Ops, SparseCore 0:
  53.8 61.6 all-reduce.2
where the time goes:
time: 285 us
  other arithmetic  80.7 us (28%)
  blocking collectives  78.2 us (27%)
  waiting for transfers between devices  60 us (21%)
  local copies, waits for them, and re-layouts  46.5 us (16%)
  between operations  14.2 us (5%)
  matrix products  5.35 us (2%)
    unnamed x1, other arithmetic  74.5 us
    unnamed x2, waiting for transfers between devices  60 us
    all_to_all x1, blocking collectives, body(): lax.all_to_all(spectra, 'wide', split_axis=0, concat_axis=2, tiled=True)  35.2 us
    unnamed x11, local copies, waits for them, and re-layouts  25.2 us
    all_to_all x1, blocking collectives, body(): lax.all_to_all(flat, 'wide', split_axis=2, concat_axis=0, tiled=True)  24.9 us
    all_to_all x1, blocking collectives, body(): lax.all_to_all(degree_part, 'wide', split_axis=0, concat_axis=1, tiled=True)  18.1 us
    reshape x1, local copies, waits for them, and re-layouts, body(): flat = summed.reshape(own_harms, 2, radii // groups * radii)  12 us
  transfers between devices with their start and end apart: 1, of which 1 were waited for; matrix products, arithmetic and copies ran while one was open for 0% of the time, Pallas kernels for 0%

commit v1 on v0

--- a/solution.py
+++ b/solution.py
@@ -1,10 +1,27 @@
+import functools
 import math
 import jax
 import jax.numpy as jnp
 from jax import lax
 from jax.sharding import PartitionSpec as P
+from jax.lax import all_to_all, axis_size
 
 HARMS = 128
+
+
+def _open_floor(work_x, mesh_dim, in_dim, dim_no):
+    return jnp.concatenate(
+        all_to_all(
+            jnp.stack(jnp.split(work_x, axis_size(mesh_dim), axis=in_dim)),
+            axis_name=mesh_dim,
+            split_axis=0,
+            concat_axis=0,
+        ),
+        axis=dim_no,
+    )
+
+
+build_types = functools.partial(_open_floor, mesh_dim="wide", in_dim=2, dim_no=0)
 
 
 def harmonic_rows(points, count):
@@ -41,7 +58,7 @@
     groups = lax.axis_size("grp")
     summed = lax.psum_scatter(corr, "grp", scatter_dimension=2, tiled=True)
     flat = summed.reshape(own_harms, 2, radii // groups * radii)
-    every_harm = lax.all_to_all(flat, "wide", split_axis=2, concat_axis=0, tiled=True)
+    every_harm = build_types(flat)
     degree_part = invert_harms(every_harm, legendre_real, legendre_imag)
     mine = lax.all_to_all(degree_part, "wide", split_axis=0, concat_axis=1, tiled=True)
     inverted = mine.reshape(own_degrees, radii // groups, radii)

time: 285 us -> 171 us (0.60)
  other arithmetic: 80.7 us -> 5.34 us
  local copies, waits for them, and re-layouts: 46.5 us -> 7.41 us
    unnamed x1 -> x0, other arithmetic: 74.5 us -> none
    unnamed x11 -> x135, local copies, waits for them, and re-layouts: 25.2 us -> 3.32 us
    reshape x1 -> x0, local copies, waits for them, and re-layouts: 12 us -> none  [body(): flat = summed.reshape(own_harms, 2, radii // groups * radii)]
    all_to_all x1 -> x0, local copies, waits for them, and re-layouts: 5.25 us -> none  [body(): lax.all_to_all(flat, 'wide', split_axis=2, concat_axis=0, tiled=True)]
  transfers between devices with their start and end apart: 1 -> 1, of which waited for: 1 -> 1; matrix products, arithmetic and copies ran while one was open for 0% -> 1% of each run, Pallas kernels for 0% -> 0%
where the time goes in v1:
time: 171 us
  blocking collectives  78.2 us (46%)
  waiting for transfers between devices  60 us (35%)
  between operations  14.6 us (9%)
  local copies, waits for them, and re-layouts  7.41 us (4%)
  other arithmetic  5.34 us (3%)
  matrix products  5.34 us (3%)
    unnamed x2, waiting for transfers between devices  60 us
    all_to_all x1, blocking collectives, body(): lax.all_to_all(spectra, 'wide', split_axis=0, concat_axis=2, tiled=True)  35.2 us
    all_to_all x1, blocking collectives, _open_floor(): all_to_all(jnp.stack(jnp.split(work_x, axis_size(mesh_dim), axis=in_dim))...  24.9 us
    all_to_all x1, blocking collectives, body(): lax.all_to_all(degree_part, 'wide', split_axis=0, concat_axis=1, tiled=True)  18.1 us
    another operation x1, other arithmetic  4.33 us
    dot_general x1, matrix products, body(): lax.dot_general(table_rows, flat_images, (((1,), (1,)), ((), ())), prefer...  3.47 us
  transfers between devices with their start and end apart: 1, of which 1 were waited for; matrix products, arithmetic and copies ran while one was open for 1% of the time, Pallas kernels for 0%

profile of v1, /device:TPU:2, one launch (start us, length us, event | category | flops | bytes accessed | tf_op | source)
XLA Modules:
  0.0 170.9 jit_solution(9521124109590117961)
XLA Ops:
  6.5 0.0 copy-start
  6.5 0.0 all-reduce.3.cloned.1.call-start
  6.5 4.3 %multiply_convert_fusion = (bf16[128,1,2048]{2,0,1:T(8,128)(2,1)S(1)}, bf16[128,1,2048]{2,0,1:T(8,128)(2,1)S(1)}) fusion(), kind=kLoop, calls=%fused_computation.12 | loop fusion | flops 4980736 | bytes 1048576 | tf_op jit(solution)/shard_map/convert.1
  10.9 0.1 pad_maximum_fusion
  11.0 1.1 copy.31
  12.1 0.4 convert_element_type.30
  12.5 3.5 %convolution_convert_fusion = bf16[256,1024]{1,0:T(8,128)(2,1)S(1)} fusion(bf16[256,2048]{1,0:T(8,128)(2,1)S(1)} %convert_element_type.30, bf16[1024,2048]{1,0:T(8,128)(2,1)} %bitcast.704), kind=kOutput, calls=%fused_computation.4 | convolution fusion | flops 1074003968 | bytes 5767168 | tf_op jit(solution)/shard_map/dot_general | solution.py:46
  16.0 0.4 reshape.179
  16.4 35.2 %all_to_all.33 = bf16[128,2,4,256]{3,2,1,0:T(4,128)(2,1)S(1)} all-to-all(bf16[128,2,4,256]{3,2,1,0:T(4,128)(2,1)S(1)} %reshape.179), channel_id=1, replica_groups=mesh['grp'=4,'wide'=128] {'wide'}, dimensions={0} | all-to-all | bytes 1048576 | tf_op jit(solution)/shard_map/all_to_all | solution.py:50
  51.6 0.0 copy-start.1
  51.6 0.0 copy-start.2
  51.6 0.5 copy.41
  52.0 0.5 convolution_bitcast_fusion
  52.6 1.0 copy.37
  53.6 0.0 all-reduce.3.cloned.1.call-update
  53.7 1.3 dynamic-slice
  55.6 59.9 %all-reduce.3.cloned.1.call-done = f32[1,2,256,256]{3,1,0,2:T(2,128)} async-done(((f32[1,2,256,256]{3,1,0,2:T(2,128)}), f32[1,2,256,256]{3,1,0,2:T(2,128)}) %all-reduce.3.cloned.1.call-update) | async-done | bytes 524304
  115.5 0.9 constant_dynamic-slice_fusion
  118.0 24.9 %all_to_all.34 = f32[128,1,2,128]{3,2,1,0:T(2,128)S(1)} all-to-all(f32[128,1,2,128]{3,2,1,0:T(2,128)S(1)} %constant_dynamic-update-slice_fusion), channel_id=1, replica_groups=mesh['grp'=4,'wide'=128] {'wide'}, dimensions={0} | all-to-all | bytes 262144 | tf_op jit(solution)/shard_map/all_to_all | solution.py:14
  142.9 0.1 fusion.16
  143.0 0.0 copy-done.1
  143.0 0.3 fusion.17
  143.3 0.0 copy-done.2
  143.3 0.3 fusion
  143.6 0.1 copy.38
  143.7 18.1 %all_to_all.35 = f32[128,1,128]{2,1,0:T(1,128)S(1)} all-to-all(f32[128,1,128]{2,1,0:T(1,128)S(1)} %copy.38), channel_id=1, replica_groups=mesh['grp'=4,'wide'=128] {'wide'}, dimensions={0} | all-to-all | bytes 131072 | tf_op jit(solution)/shard_map/all_to_all | solution.py:63
  161.8 0.5 broadcast.137
  162.4 0.8 reduce.3
  163.2 0.0 copy-done
  163.2 0.8 convolution_bitcast_fusion.1
  (132 shorter events, 1.3 us)
Async XLA Ops:
  6.5 156.7 %copy-start = (f32[1,256,128]{2,1,0:T(8,128)S(1)}, f32[1,256,128]{2,1,0:T(8,128)}, u32[]{:S(2)}) copy-start(f32[1,256,128]{2,1,0:T(8,128)} %param.7) | copy-start | bytes 393220
  6.5 109.0 %all-reduce.3.cloned.1.call-start = ((), (), s32[]{:S(2)}) async-start(), calls=%async_computation.3 | async-start | bytes 1048576
  51.6 91.4 %copy-start.1 = (f32[128,128]{1,0:T(8,128)S(1)}, f32[128,128]{1,0:T(8,128)}, u32[]{:S(2)}) copy-start(f32[128,128]{1,0:T(8,128)} %param.5) | copy-start | bytes 196612
  51.6 91.7 %copy-start.2 = (f32[128,128]{1,0:T(8,128)S(1)}, f32[128,128]{1,0:T(8,128)}, u32[]{:S(2)}) copy-start(f32[128,128]{1,0:T(8,128)} %param.6) | copy-start | bytes 196612
Sparse Core Ops, SparseCore 0:
  53.8 61.6 all-reduce.2
